TPU v7x, 32 devices: a whole 2x2x4 slice. The times are simulated.
32 devices in a mesh: stn: 8 (over z, core), chan: 4 (over y, x).
Axes of the slice: x: 2, y: 2, z: 4, core: 2. Of those that a mesh axis runs over, the one named last changes fastest.
Arguments:
- voltages: bfloat16 [64, 32, 2, 1024], P('stn', 'chan'), may hold values from -6 to 6
- filter_taps: float32 [16, 1024], replicated, may hold values from -1.5 to 1.5
Outputs:
- visibilities: bfloat16 [1024, 2, 64, 64], P('chan', None, 'stn')
All inputs are finite; a program needn't handle non-finite values.
Results may differ from a plain program's by a relative error of at most 0.0069.
Values may be sent and summed in bfloat16 or wider, within the bound.
A program may use at most 64 MiB of HBM per device.

v0:
```python
import math
import jax
import jax.numpy as jnp
from jax import lax
from jax.sharding import PartitionSpec as P


def from_behind(array, axis, by):
    devices = lax.axis_size(axis)
    pairs = [(i, i + by) for i in range(devices) if 0 <= i + by < devices]
    return lax.ppermute(array, axis, pairs)


def passed_along(value, axis, steps):
    count = lax.axis_size(axis)
    pairs = [(source, (source + steps) % count) for source in range(count)]
    return lax.ppermute(value, axis, pairs)


def fourier_matrix(points):
    sample_index = jnp.arange(points, dtype=jnp.int32)
    phase = sample_index[:, None] * sample_index[None, :] % points
    angle = phase.astype(jnp.float32) * (2.0 * math.pi / points)
    norm_factor = 1.0 / math.sqrt(points)
    cosine = (jnp.cos(angle) * norm_factor).astype(jnp.bfloat16)
    sine_part = (-jnp.sin(angle) * norm_factor).astype(jnp.bfloat16)
    upper_rows = jnp.stack([cosine, sine_part], axis=2)
    lower_rows = jnp.stack([-sine_part, cosine], axis=2)
    return jnp.concatenate([upper_rows, lower_rows], axis=0).reshape(2 * points, 2 * points)


def history_frames(voltages, history_len):
    frames_here = voltages.shape[1]
    shift_count = (history_len - 1) // frames_here + 1
    earlier = []
    for distance in range(1, shift_count + 1):
        keep_count = min(frames_here, history_len - (distance - 1) * frames_here)
        received_frames = from_behind(voltages[:, frames_here - keep_count :], "chan", distance)
        earlier = [received_frames] + earlier
    return jnp.concatenate(earlier + [voltages], axis=1)


def correlate(local_block, swapped, other_block, factor):
    real_part = jnp.einsum(
        "kcas,kcbs->kab", local_block, other_block, preferred_element_type=jnp.float32
    )
    imag_part = jnp.einsum(
        "kcas,kcbs->kab", swapped, other_block, preferred_element_type=jnp.float32
    )
    return jnp.stack([real_part, imag_part], axis=1) * factor


def mirrored(product):
    return jnp.stack(
        [jnp.swapaxes(product[:, 0], 1, 2), -jnp.swapaxes(product[:, 1], 1, 2)], axis=1
    )


def place_block(buffer, product, chan_start, slot_index):
    columns = product.shape[3]
    anchor = jnp.int32(0)
    return lax.dynamic_update_slice(
        buffer, product, (jnp.int32(chan_start), anchor, anchor, slot_index * columns)
    )


def per_device(voltages, filter_taps):
    inputs_here, frames_here, parts, points = voltages.shape
    tap_count = filter_taps.shape[0]
    extended = history_frames(voltages, tap_count - 1)
    filtered = jnp.zeros(voltages.shape, jnp.float32)
    for tap_index in range(tap_count):
        offset = tap_count - 1 - tap_index
        filtered = filtered + filter_taps[tap_index][None, None, None, :] * extended[
            :, offset : offset + frames_here
        ].astype(jnp.float32)
    filtered = filtered.astype(jnp.bfloat16).reshape(inputs_here, frames_here, parts * points)
    matrix = fourier_matrix(points)
    spectra = jnp.einsum("isr,rq->qis", filtered, matrix, preferred_element_type=jnp.float32)
    spectra = spectra.reshape(points, parts, inputs_here, frames_here).astype(jnp.bfloat16)
    local_block = lax.all_to_all(spectra, "chan", split_axis=0, concat_axis=3, tiled=True)
    cycle_size = lax.axis_size("stn")
    position = lax.axis_index("stn")
    halfway = cycle_size // 2
    channels = local_block.shape[0]
    factor = 1.0 / local_block.shape[3]
    swapped = jnp.stack([local_block[:, 1], -local_block[:, 0]], axis=1)
    row_sums = jnp.zeros((channels, parts, inputs_here, cycle_size * inputs_here), jnp.float32)
    row_sums = place_block(
        row_sums, correlate(local_block, swapped, local_block, factor), 0, position
    )
    mirror = jnp.zeros(row_sums.shape, jnp.bfloat16)

    def cycle_turn(step_index, carry):
        moving_block, row_sums, mirror = carry
        moving_block = passed_along(moving_block, "stn", -1)
        slot_index = (position + step_index) % cycle_size
        is_kept = jnp.logical_or(step_index < halfway, position < halfway)
        product = jnp.where(is_kept, correlate(local_block, swapped, moving_block, factor), 0.0)
        row_sums = place_block(row_sums, product, 0, slot_index)
        outgoing = mirrored(product).astype(jnp.bfloat16)
        mirror = place_block(mirror, outgoing, 0, slot_index)
        return (moving_block, row_sums, mirror)

    moving_block, row_sums, mirror = lax.fori_loop(
        1, halfway + 1, cycle_turn, (local_block, row_sums, mirror)
    )
    returned = lax.all_to_all(mirror, "stn", split_axis=3, concat_axis=3, tiled=True)
    row_sums = row_sums + returned.astype(jnp.float32)
    return row_sums.astype(jnp.bfloat16)


def solution(mesh):
    placed = (P("stn", "chan", None, None), P())
    return jax.shard_map(
        per_device,
        mesh=mesh,
        in_specs=placed,
        out_specs=P("chan", None, "stn", None),
        check_vma=False,
    )
```

profile of v0, /device:TPU:0, one launch (start us, length us, event | category | flops | bytes accessed | tf_op | source)
XLA Modules:
  0.0 217.8 jit_solution(14949994201829251121)
XLA Ops:
  0.0 4.8 %collective-permute-start.1 = (bf16[8,8,2,1024]{3,2,1,0:T(2,128)(2,1)}, bf16[8,8,2,1024]{3,2,1,0:T(2,128)(2,1)S(1)}, u32[]{:S(2)}, u32[]{:S(2)}) collective-permute-start(bf16[8,8,2,1024]{3,2,1,0:T(2,128)(2,1)} %param.4), channel_id=1, source_target_pairs={{0,1},{1,2},{2,3},{4,5},{5,6},{6,7},{8,9},{9,10},{10,11},{12,13},{... | collective-permute-start | bytes 786440 | tf_op jit(solution)/shard_map/ppermute | solution.py:11
  9.4 17.1 %multiply_convert_fusion = (bf16[1024,1024,1]{1,0,2:T(8,128)(2,1)S(1)}, bf16[1024,1024,1]{1,0,2:T(8,128)(2,1)S(1)}) fusion(), kind=kLoop, calls=%fused_computation.21 | loop fusion | flops 19922944 | bytes 4194304 | tf_op jit(solution)/shard_map/convert_element_type | solution.py:26
  26.6 15.8 %fusion.16 = bf16[1024,1024,1]{1,0,2:T(8,128)(2,1)S(1)} fusion(), kind=kLoop, calls=%fused_computation.31 | loop fusion | flops 20971520 | bytes 2097152 | tf_op jit(solution)/shard_map/neg | solution.py:28
  42.4 4.0 %maximum_maximum_fusion = bf16[2048,1024,2]{1,0,2:T(8,128)(2,1)} fusion(bf16[1024,1024,1]{1,0,2:T(8,128)(2,1)S(1)} %get-tuple-element.262, bf16[1024,1024,1]{1,0,2:T(8,128)(2,1)S(1)} %fusion.16, bf16[1024,1024,1]{1,0,2:T(8,128)(2,1)S(1)} %get-tuple-element.261), kind=kLoop, calls=%fused_computation.12 | loop fusion | flops 33554432 | bytes 14680064 | tf_op jit(solution)/shard_map/concatenate | solution.py:29
  46.4 21.5 %copy.62 = bf16[2048,1024,2]{0,2,1:T(2,128)(2,1)} copy(bf16[2048,1024,2]{1,0,2:T(8,128)(2,1)} %maximum_maximum_fusion) | data formatting | bytes 16777216 | tf_op jit(solution)/shard_map/concatenate | solution.py:29
  67.9 13.1 %reshape.119 = bf16[2048,2048]{0,1:T(8,128)(2,1)} reshape(bf16[2048,1024,2]{0,2,1:T(2,128)(2,1)} %copy.62) | data formatting | bytes 16777216 | tf_op jit(solution)/shard_map/reshape | solution.py:29
  81.0 14.2 %dot_general.34 = bf16[1024,2,2048]{2,1,0:T(2,128)(2,1)} reshape(bf16[2048,2048]{1,0:T(8,128)(2,1)} %bitcast.78) | data formatting | bytes 16777216 | tf_op jit(solution)/shard_map/isr,rq->qis/dot_general | solution.py:79
  96.0 3.8 %add_convert_fusion = bf16[8,8,2,1024]{3,2,1,0:T(2,128)(2,1)S(1)} fusion(bf16[8,8,2,1024]{3,2,1,0:T(2,128)(2,1)S(1)} %collective-permute-done.1, bf16[8,8,2,1024]{3,2,1,0:T(2,128)(2,1)S(1)} %copy-done.1, bf16[8,15,2,1024]{3,2,1,0:T(2,128)(2,1)S(1)} %get-tuple-element.244, bf16[8,16,2,1024]{3,2,1,0:T(2,128)(2,1)S(1)} %constant_dynamic-update-slice_fusion.1, ...), kind=kLoop, calls=%fused_computation.32 | loop fusion | flops 6291456 | bytes 4521984 | tf_op jit(solution)/shard_map/convert_element_type | solution.py:77
  100.0 8.2 %fusion.12 = bf16[1024,2,8,8]{0,3,2,1:T(8,128)(2,1)S(1)} fusion(bf16[8,8,2048,1]{2,1,0,3:T(8,128)(2,1)S(1)} %reshape.124, bf16[1024,2,2048,1]{2,1,0,3:T(2,128)(2,1)} %bitcast.80), kind=kOutput, calls=%fused_computation.28 | convolution fusion | flops 537001984 | bytes 8912896 | tf_op jit(solution)/shard_map/isr,rq->qis/dot_general | solution.py:79
  108.3 4.7 %copy.64 = bf16[1024,2,8,8]{3,2,1,0:T(8,128)(2,1)} copy(bf16[1024,2,8,8]{0,3,2,1:T(8,128)(2,1)S(1)} %fusion.12) | data formatting | bytes 524288 | tf_op jit(solution)/shard_map/convert_element_type | solution.py:80
  113.0 6.4 %reshape.128 = bf16[4,2,16384]{2,1,0:T(2,128)(2,1)} reshape(bf16[1024,2,8,8]{3,2,1,0:T(8,128)(2,1)} %copy.64) | data formatting | bytes 524288
  119.4 3.4 %all-to-all-start = ((bf16[4,2,16384]{2,1,0:T(2,128)(2,1)}), bf16[4,2,16384]{2,1,0:T(2,128)(2,1)S(1)}, u32[]{:S(2)}, u32[]{:S(2)}) async-start(bf16[4,2,16384]{2,1,0:T(2,128)(2,1)} %reshape.128), calls=%async_computation | async-start | bytes 524288 | tf_op jit(solution)/shard_map/all_to_all | solution.py:81
  122.8 5.3 %all-to-all-done = bf16[4,2,16384]{2,1,0:T(2,128)(2,1)S(1)} async-done(((bf16[4,2,16384]{2,1,0:T(2,128)(2,1)}), bf16[4,2,16384]{2,1,0:T(2,128)(2,1)S(1)}, u32[]{:S(2)}, u32[]{:S(2)}) %all-to-all-start) | async-done | bytes 262176 | tf_op jit(solution)/shard_map/all_to_all | solution.py:81
  128.1 5.9 %reshape.129 = bf16[1024,2,8,8]{3,2,1,0:T(8,128)(2,1)} reshape(bf16[4,2,16384]{2,1,0:T(2,128)(2,1)S(1)} %all-to-all-done) | data formatting | bytes 524288
  134.1 4.7 %copy.85 = bf16[4,256,2,8,8]{1,0,4,3,2:T(4,128)(2,1)S(1)} copy(bf16[4,256,2,8,8]{4,3,2,1,0:T(8,128)(2,1)} %bitcast.79) | data formatting | bytes 524288 | tf_op jit(solution)/shard_map/all_to_all | solution.py:81
  145.8 48.9 %while.19 = (s32[]{:T(128)}, bf16[256,2,8,32]{0,3,2,1:T(8,128)(2,1)S(1)}, f32[256,2,8,64]{0,3,2,1:T(8,128)}, bf16[256,2,8,64]{0,2,1,3:T(8,128)(2,1)}, pred[]{:T(...) while((s32[]{:T(128)}, ...), condition=%wide.region_1.2_spmd, body=%wide.region_0.1_spmd.sunk | while | flops 4358164 | bytes 4489577 | solution.py:105
  147.1 3.9 %collective-permute-done = bf16[256,2,8,32]{0,3,2,1:T(8,128)(2,1)S(1)} collective-permute-done((bf16[256,2,8,32]{0,3,2,1:T(8,128)(2,1)S(1)}, bf16[256,2,8,32]{0,3,2,1:T(8,128)(2,1)S(1)}, u32[]{:S(2)}, u32[]{:S(2)}) %collective-permute-start) | collective-permute-done | bytes 262176 | tf_op jit(solution)/shard_map/while/body/eval_jaxpr/ppermute | solution.py:17
  156.2 3.8 %collective-permute-start = (bf16[256,2,8,32]{0,3,2,1:T(8,128)(2,1)S(1)}, bf16[256,2,8,32]{0,3,2,1:T(8,128)(2,1)S(1)}, u32[]{:S(2)}, u32[]{:S(2)}) collective-permute-start(bf16[256,2,8,32]{0,3,2,1:T(8,128)(2,1)S(1)} %get-tuple-element.331), channel_id=1, source_target_pairs={{0,28},{4,0},{8,4},{12,8},{16,12},{20,16},{24,20},{28,24},{1,29},{... | collective-permute-start | bytes 786440 | tf_op jit(solution)/shard_map/while/body/eval_jaxpr/ppermute | solution.py:17
  160.0 3.9 %collective-permute-done = bf16[256,2,8,32]{0,3,2,1:T(8,128)(2,1)S(1)} collective-permute-done((bf16[256,2,8,32]{0,3,2,1:T(8,128)(2,1)S(1)}, bf16[256,2,8,32]{0,3,2,1:T(8,128)(2,1)S(1)}, u32[]{:S(2)}, u32[]{:S(2)}) %collective-permute-start) | collective-permute-done | bytes 262176 | tf_op jit(solution)/shard_map/while/body/eval_jaxpr/ppermute | solution.py:17
  169.0 3.8 %collective-permute-start = (bf16[256,2,8,32]{0,3,2,1:T(8,128)(2,1)S(1)}, bf16[256,2,8,32]{0,3,2,1:T(8,128)(2,1)S(1)}, u32[]{:S(2)}, u32[]{:S(2)}) collective-permute-start(bf16[256,2,8,32]{0,3,2,1:T(8,128)(2,1)S(1)} %get-tuple-element.331), channel_id=1, source_target_pairs={{0,28},{4,0},{8,4},{12,8},{16,12},{20,16},{24,20},{28,24},{1,29},{... | collective-permute-start | bytes 786440 | tf_op jit(solution)/shard_map/while/body/eval_jaxpr/ppermute | solution.py:17
  172.8 3.9 %collective-permute-done = bf16[256,2,8,32]{0,3,2,1:T(8,128)(2,1)S(1)} collective-permute-done((bf16[256,2,8,32]{0,3,2,1:T(8,128)(2,1)S(1)}, bf16[256,2,8,32]{0,3,2,1:T(8,128)(2,1)S(1)}, u32[]{:S(2)}, u32[]{:S(2)}) %collective-permute-start) | collective-permute-done | bytes 262176 | tf_op jit(solution)/shard_map/while/body/eval_jaxpr/ppermute | solution.py:17
  181.9 3.7 %collective-permute-start = (bf16[256,2,8,32]{0,3,2,1:T(8,128)(2,1)S(1)}, bf16[256,2,8,32]{0,3,2,1:T(8,128)(2,1)S(1)}, u32[]{:S(2)}, u32[]{:S(2)}) collective-permute-start(bf16[256,2,8,32]{0,3,2,1:T(8,128)(2,1)S(1)} %get-tuple-element.331), channel_id=1, source_target_pairs={{0,28},{4,0},{8,4},{12,8},{16,12},{20,16},{24,20},{28,24},{1,29},{... | collective-permute-start | bytes 786440 | tf_op jit(solution)/shard_map/while/body/eval_jaxpr/ppermute | solution.py:17
  185.6 3.9 %collective-permute-done = bf16[256,2,8,32]{0,3,2,1:T(8,128)(2,1)S(1)} collective-permute-done((bf16[256,2,8,32]{0,3,2,1:T(8,128)(2,1)S(1)}, bf16[256,2,8,32]{0,3,2,1:T(8,128)(2,1)S(1)}, u32[]{:S(2)}, u32[]{:S(2)}) %collective-permute-start) | collective-permute-done | bytes 262176 | tf_op jit(solution)/shard_map/while/body/eval_jaxpr/ppermute | solution.py:17
  194.7 20.3 %all_to_all.23 = bf16[256,2,8,64]{0,2,1,3:T(8,128)(2,1)S(1)} all-to-all(bf16[256,2,8,64]{0,2,1,3:T(8,128)(2,1)} %get-tuple-element.190), channel_id=1, replica_groups=mesh['stn'=8,'chan'=4] {'stn'}, dimensions={3} | all-to-all | bytes 1048576 | tf_op jit(solution)/shard_map/all_to_all | solution.py:108
  (82 shorter events, 37.1 us)
Async XLA Ops:
  0.0 95.4 %collective-permute-start.1 = (bf16[8,8,2,1024]{3,2,1,0:T(2,128)(2,1)}, bf16[8,8,2,1024]{3,2,1,0:T(2,128)(2,1)S(1)}, u32[]{:S(2)}, u32[]{:S(2)}) collective-permute-start(bf16[8,8,2,1024]{3,2,1,0:T(2,128)(2,1)} %param.4), channel_id=1, source_target_pairs={{0,1},{1,2},{2,3},{4,5},{5,6},{6,7},{8,9},{9,10},{10,11},{12,13},{... | collective-permute-start | bytes 786440 | tf_op jit(solution)/shard_map/ppermute | solution.py:11
  6.0 89.2 %collective-permute-start.2 = (bf16[8,7,2,1024]{3,2,1,0:T(2,128)(2,1)S(1)}, bf16[8,7,2,1024]{3,2,1,0:T(2,128)(2,1)S(1)}, u32[]{:S(2)}, u32[]{:S(2)}) collective-permute-start(bf16[8,7,2,1024]{3,2,1,0:T(2,128)(2,1)S(1)} %slice.151), channel_id=1, source_target_pairs={{0,2},{1,3},{4,6},{5,7},{8,10},{9,11},{12,14},{13,15},{16,18},{17,... | collective-permute-start | bytes 688136 | tf_op jit(solution)/shard_map/ppermute | solution.py:11
  81.0 14.2 %copy-start.2 = (f32[16,1024]{1,0:T(8,128)S(1)}, f32[16,1024]{1,0:T(8,128)}, u32[]{:S(2)}) copy-start(f32[16,1024]{1,0:T(8,128)} %param.5) | copy-start | bytes 196612
  81.0 14.8 %copy-start.1 = (bf16[8,8,2,1024]{3,2,1,0:T(2,128)(2,1)S(1)}, bf16[8,8,2,1024]{3,2,1,0:T(2,128)(2,1)}, u32[]{:S(2)}) copy-start(bf16[8,8,2,1024]{3,2,1,0:T(2,128)(2,1)} %param.4) | copy-start | bytes 786436
  119.4 8.8 %all-to-all-start = ((bf16[4,2,16384]{2,1,0:T(2,128)(2,1)}), bf16[4,2,16384]{2,1,0:T(2,128)(2,1)S(1)}, u32[]{:S(2)}, u32[]{:S(2)}) async-start(bf16[4,2,16384]{2,1,0:T(2,128)(2,1)} %reshape.128), calls=%async_computation | async-start | bytes 524288 | tf_op jit(solution)/shard_map/all_to_all | solution.py:81
  144.6 1.2 copy-start
  145.8 5.2 %collective-permute-start = (bf16[256,2,8,32]{0,3,2,1:T(8,128)(2,1)S(1)}, bf16[256,2,8,32]{0,3,2,1:T(8,128)(2,1)S(1)}, u32[]{:S(2)}, u32[]{:S(2)}) collective-permute-start(bf16[256,2,8,32]{0,3,2,1:T(8,128)(2,1)S(1)} %get-tuple-element.331), channel_id=1, source_target_pairs={{0,28},{4,0},{8,4},{12,8},{16,12},{20,16},{24,20},{28,24},{1,29},{... | collective-permute-start | bytes 786440 | tf_op jit(solution)/shard_map/while/body/eval_jaxpr/ppermute | solution.py:17
  156.2 7.7 %collective-permute-start = (bf16[256,2,8,32]{0,3,2,1:T(8,128)(2,1)S(1)}, bf16[256,2,8,32]{0,3,2,1:T(8,128)(2,1)S(1)}, u32[]{:S(2)}, u32[]{:S(2)}) collective-permute-start(bf16[256,2,8,32]{0,3,2,1:T(8,128)(2,1)S(1)} %get-tuple-element.331), channel_id=1, source_target_pairs={{0,28},{4,0},{8,4},{12,8},{16,12},{20,16},{24,20},{28,24},{1,29},{... | collective-permute-start | bytes 786440 | tf_op jit(solution)/shard_map/while/body/eval_jaxpr/ppermute | solution.py:17
  169.0 7.7 %collective-permute-start = (bf16[256,2,8,32]{0,3,2,1:T(8,128)(2,1)S(1)}, bf16[256,2,8,32]{0,3,2,1:T(8,128)(2,1)S(1)}, u32[]{:S(2)}, u32[]{:S(2)}) collective-permute-start(bf16[256,2,8,32]{0,3,2,1:T(8,128)(2,1)S(1)} %get-tuple-element.331), channel_id=1, source_target_pairs={{0,28},{4,0},{8,4},{12,8},{16,12},{20,16},{24,20},{28,24},{1,29},{... | collective-permute-start | bytes 786440 | tf_op jit(solution)/shard_map/while/body/eval_jaxpr/ppermute | solution.py:17
  181.9 7.6 %collective-permute-start = (bf16[256,2,8,32]{0,3,2,1:T(8,128)(2,1)S(1)}, bf16[256,2,8,32]{0,3,2,1:T(8,128)(2,1)S(1)}, u32[]{:S(2)}, u32[]{:S(2)}) collective-permute-start(bf16[256,2,8,32]{0,3,2,1:T(8,128)(2,1)S(1)} %get-tuple-element.331), channel_id=1, source_target_pairs={{0,28},{4,0},{8,4},{12,8},{16,12},{20,16},{24,20},{28,24},{1,29},{... | collective-permute-start | bytes 786440 | tf_op jit(solution)/shard_map/while/body/eval_jaxpr/ppermute | solution.py:17
where the time goes:
time: 220 us; the launch traced here: 218 us
  local copies, waits for them, and re-layouts  87.8 us (40%)
  other arithmetic  45.6 us (21%)
  starting transfers between devices  24.3 us (11%)
  waiting for transfers between devices  20.9 us (10%)
  blocking collectives  20.3 us (9%)
  matrix products  18.5 us (8%)
    concatenate x1, local copies, waits for them, and re-layouts, fourier_matrix(): jnp.concatenate([upper_rows, lower_rows], axis=0)  21.5 us
    all_to_all x1, blocking collectives, per_device(): lax.all_to_all(mirror, 'stn', split_axis=3, concat_axis=3, tiled=True)  20.3 us
    convert_element_type x1, other arithmetic, fourier_matrix(): sine_part = (-jnp.sin(angle) * norm_factor).astype(jnp.bfloat16)  17.1 us
    neg x1, other arithmetic, fourier_matrix(): lower_rows = jnp.stack([-sine_part, cosine], axis=2)  15.8 us
    ppermute x4, waiting for transfers between devices, passed_along(): return lax.ppermute(value, axis, pairs)  15.6 us
    dot_general x1, local copies, waits for them, and re-layouts, per_device(): jnp.einsum('isr,rq->qis', filtered, matrix, preferred_element_type=jnp.fl...  14.2 us
    unnamed x10, local copies, waits for them, and re-layouts  13.2 us
    reshape x1, local copies, waits for them, and re-layouts, fourier_matrix(): jnp.concatenate([upper_rows, lower_rows], axis=0)  13.1 us
  transfers between devices with their start and end apart: 7, of which 5 were waited for; matrix products, arithmetic and copies ran while one was open for 40% of the time, Pallas kernels for 0%

commit v1 on v0

--- a/solution.py
+++ b/solution.py
@@ -3,6 +3,20 @@
 import jax.numpy as jnp
 from jax import lax
 from jax.sharding import PartitionSpec as P
+
+
+def _extend_seats_all(z, ndim_at, obj):
+    near = z.shape
+    u1 = z.reshape(*near[:ndim_at], obj, near[ndim_at] // obj, *near[ndim_at + 1 :])
+    f_now = jnp.moveaxis(u1, ndim_at, 0)
+    return f_now
+
+
+def fill_the_yards(panel, dim_at):
+    then = list(panel.shape[1:])
+    then[dim_at] *= panel.shape[0]
+    shaped = jnp.moveaxis(panel, 0, dim_at).reshape(then)
+    return shaped
 
 
 def from_behind(array, axis, by):
@@ -105,7 +119,14 @@
     moving_block, row_sums, mirror = lax.fori_loop(
         1, halfway + 1, cycle_turn, (local_block, row_sums, mirror)
     )
-    returned = lax.all_to_all(mirror, "stn", split_axis=3, concat_axis=3, tiled=True)
+    new, finding = (jax.lax.axis_size("stn"), jax.lax.axis_index("stn"))
+    v1 = _extend_seats_all(mirror, 3, new)
+    series = [v1[finding]]
+    for d in tuple(range(1, new)):
+        w_next = v1[(finding + d) % new]
+        series.append(jax.lax.ppermute(w_next, "stn", [(pp, (pp + d) % new) for pp in range(new)]))
+    v1 = jnp.stack(series, 0)[(finding - jnp.arange(new)) % new]
+    returned = fill_the_yards(v1, 3)
     row_sums = row_sums + returned.astype(jnp.float32)
     return row_sums.astype(jnp.bfloat16)
 

time: 220 us -> 218 us (level)
  blocking collectives: 20.3 us -> 0 us
  starting transfers between devices: 24.3 us -> 32.5 us
  other arithmetic: 45.6 us -> 51.3 us
  waiting for transfers between devices: 20.9 us -> 26.1 us
    all_to_all x1 -> x0, blocking collectives: 20.3 us -> none  [per_device(): lax.all_to_all(mirror, 'stn', split_axis=3, concat_axis=3, tiled=True)]
    ppermute x0 -> x7, starting transfers between devices: none -> 8.29 us  [per_device(): jax.lax.ppermute(w_next, 'stn', [(pp, (pp + d) % new) for pp in range(new)])]
    ppermute x0 -> x7, waiting for transfers between devices: none -> 5.2 us  [per_device(): jax.lax.ppermute(w_next, 'stn', [(pp, (pp + d) % new) for pp in range(new)])]
    dynamic_update_slice x5 -> x9, other arithmetic: 2.84 us -> 5.51 us  [place_block(): lax.dynamic_update_slice(buffer, product, (jnp.int32(chan_start), anchor,...]
    dynamic_update_slice x4 -> x0, local copies, waits for them, and re-layouts: 2.6 us -> none  [place_block(): lax.dynamic_update_slice(buffer, product, (jnp.int32(chan_start), anchor,...]
    concatenate x1, other arithmetic: 4.04 us -> 6.57 us  [fourier_matrix(): jnp.concatenate([upper_rows, lower_rows], axis=0)]
    unnamed x10 -> x19, local copies, waits for them, and re-layouts: 13.2 us -> 14.6 us
  transfers between devices with their start and end apart: 7 -> 14, of which waited for: 5 -> 8; matrix products, arithmetic and copies ran while one was open for 40% -> 43% of each run, Pallas kernels for 0% -> 0%
where the time goes in v1:
time: 218 us; the launch traced here: 216 us
  local copies, waits for them, and re-layouts  87.5 us (40%)
  other arithmetic  51.3 us (24%)
  starting transfers between devices  32.5 us (15%)
  waiting for transfers between devices  26.1 us (12%)
  matrix products  18.5 us (8%)
    concatenate x1, local copies, waits for them, and re-layouts, fourier_matrix(): jnp.concatenate([upper_rows, lower_rows], axis=0)  21.5 us
    convert_element_type x1, other arithmetic, fourier_matrix(): sine_part = (-jnp.sin(angle) * norm_factor).astype(jnp.bfloat16)  17.9 us
    neg x1, other arithmetic, fourier_matrix(): lower_rows = jnp.stack([-sine_part, cosine], axis=2)  16.5 us
    ppermute x4, waiting for transfers between devices, passed_along(): return lax.ppermute(value, axis, pairs)  15.6 us
    unnamed x19, local copies, waits for them, and re-layouts  14.6 us
    dot_general x1, local copies, waits for them, and re-layouts, per_device(): jnp.einsum('isr,rq->qis', filtered, matrix, preferred_element_type=jnp.fl...  14.2 us
    reshape x1, local copies, waits for them, and re-layouts, fourier_matrix(): jnp.concatenate([upper_rows, lower_rows], axis=0)  13.1 us
    ppermute x4, starting transfers between devices, passed_along(): return lax.ppermute(value, axis, pairs)  12.6 us
  transfers between devices with their start and end apart: 14, of which 8 were waited for; matrix products, arithmetic and copies ran while one was open for 43% of the time, Pallas kernels for 0%

profile of v1, /device:TPU:0, one launch (start us, length us, event | category | flops | bytes accessed | tf_op | source)
XLA Modules:
  0.0 216.4 jit_solution(13094917617574337028)
XLA Ops:
  0.0 4.8 %collective-permute-start.1 = (bf16[8,8,2,1024]{3,2,1,0:T(2,128)(2,1)}, bf16[8,8,2,1024]{3,2,1,0:T(2,128)(2,1)S(1)}, u32[]{:S(2)}, u32[]{:S(2)}) collective-permute-start(bf16[8,8,2,1024]{3,2,1,0:T(2,128)(2,1)} %param.4), channel_id=1, source_target_pairs={{0,1},{1,2},{2,3},{4,5},{5,6},{6,7},{8,9},{9,10},{10,11},{12,13},{... | collective-permute-start | bytes 786440 | tf_op jit(solution)/shard_map/ppermute | solution.py:25
  9.4 17.9 %multiply_convert_fusion = (bf16[1024,1024,1]{1,0,2:T(8,128)(2,1)S(1)}, bf16[1024,1024,1]{1,0,2:T(8,128)(2,1)}) fusion(), kind=kLoop, calls=%fused_computation.21 | loop fusion | flops 19922944 | bytes 4194304 | tf_op jit(solution)/shard_map/convert_element_type | solution.py:40
  27.3 16.5 %fusion.16 = bf16[1024,1024,1]{1,0,2:T(8,128)(2,1)} fusion(), kind=kLoop, calls=%fused_computation.32 | loop fusion | flops 20971520 | bytes 2097152 | tf_op jit(solution)/shard_map/neg | solution.py:42
  43.8 6.6 %maximum_maximum_fusion = bf16[2048,1024,2]{1,0,2:T(8,128)(2,1)} fusion(bf16[1024,1024,1]{1,0,2:T(8,128)(2,1)} %get-tuple-element.277, bf16[1024,1024,1]{1,0,2:T(8,128)(2,1)} %fusion.16, bf16[1024,1024,1]{1,0,2:T(8,128)(2,1)S(1)} %get-tuple-element.276), kind=kLoop, calls=%fused_computation.12 | loop fusion | flops 33554432 | bytes 14680064 | tf_op jit(solution)/shard_map/concatenate | solution.py:43
  50.4 21.5 %copy.98 = bf16[2048,1024,2]{0,2,1:T(2,128)(2,1)} copy(bf16[2048,1024,2]{1,0,2:T(8,128)(2,1)} %maximum_maximum_fusion) | data formatting | bytes 16777216 | tf_op jit(solution)/shard_map/concatenate | solution.py:43
  71.8 13.1 %reshape.189 = bf16[2048,2048]{0,1:T(8,128)(2,1)} reshape(bf16[2048,1024,2]{0,2,1:T(2,128)(2,1)} %copy.98) | data formatting | bytes 16777216 | tf_op jit(solution)/shard_map/reshape | solution.py:43
  85.0 14.2 %dot_general.34 = bf16[1024,2,2048]{2,1,0:T(2,128)(2,1)} reshape(bf16[2048,2048]{1,0:T(8,128)(2,1)} %bitcast.134) | data formatting | bytes 16777216 | tf_op jit(solution)/shard_map/isr,rq->qis/dot_general | solution.py:93
  100.1 3.8 %add_convert_fusion = bf16[8,8,2,1024]{3,2,1,0:T(2,128)(2,1)S(1)} fusion(bf16[8,8,2,1024]{3,2,1,0:T(2,128)(2,1)S(1)} %collective-permute-done.1, bf16[8,8,2,1024]{3,2,1,0:T(2,128)(2,1)S(1)} %copy-done.2, bf16[8,15,2,1024]{3,2,1,0:T(2,128)(2,1)S(1)} %get-tuple-element.259, bf16[8,16,2,1024]{3,2,1,0:T(2,128)(2,1)S(1)} %constant_dynamic-update-slice_fusion.1, ...), kind=kLoop, calls=%fused_computation.33 | loop fusion | flops 6291456 | bytes 4521984 | tf_op jit(solution)/shard_map/convert_element_type | solution.py:91
  104.1 8.2 %fusion.12 = bf16[1024,2,8,8]{0,3,2,1:T(8,128)(2,1)S(1)} fusion(bf16[8,8,2048,1]{2,1,0,3:T(8,128)(2,1)S(1)} %reshape.204, bf16[1024,2,2048,1]{2,1,0,3:T(2,128)(2,1)} %bitcast.136), kind=kOutput, calls=%fused_computation.28 | convolution fusion | flops 537001984 | bytes 8912896 | tf_op jit(solution)/shard_map/isr,rq->qis/dot_general | solution.py:93
  112.3 4.7 %copy.100 = bf16[1024,2,8,8]{3,2,1,0:T(8,128)(2,1)} copy(bf16[1024,2,8,8]{0,3,2,1:T(8,128)(2,1)S(1)} %fusion.12) | data formatting | bytes 524288 | tf_op jit(solution)/shard_map/convert_element_type | solution.py:94
  117.0 6.4 %reshape.208 = bf16[4,2,16384]{2,1,0:T(2,128)(2,1)} reshape(bf16[1024,2,8,8]{3,2,1,0:T(8,128)(2,1)} %copy.100) | data formatting | bytes 524288
  123.4 3.4 %all-to-all-start = ((bf16[4,2,16384]{2,1,0:T(2,128)(2,1)}), bf16[4,2,16384]{2,1,0:T(2,128)(2,1)S(1)}, u32[]{:S(2)}, u32[]{:S(2)}) async-start(bf16[4,2,16384]{2,1,0:T(2,128)(2,1)} %reshape.208), calls=%async_computation | async-start | bytes 524288 | tf_op jit(solution)/shard_map/all_to_all | solution.py:95
  126.8 5.3 %all-to-all-done = bf16[4,2,16384]{2,1,0:T(2,128)(2,1)S(1)} async-done(((bf16[4,2,16384]{2,1,0:T(2,128)(2,1)}), bf16[4,2,16384]{2,1,0:T(2,128)(2,1)S(1)}, u32[]{:S(2)}, u32[]{:S(2)}) %all-to-all-start) | async-done | bytes 262176 | tf_op jit(solution)/shard_map/all_to_all | solution.py:95
  132.1 5.9 %reshape.209 = bf16[1024,2,8,8]{3,2,1,0:T(8,128)(2,1)} reshape(bf16[4,2,16384]{2,1,0:T(2,128)(2,1)S(1)} %all-to-all-done) | data formatting | bytes 524288
  138.1 4.7 %copy.127 = bf16[4,256,2,8,8]{1,0,4,3,2:T(4,128)(2,1)S(1)} copy(bf16[4,256,2,8,8]{4,3,2,1,0:T(8,128)(2,1)} %bitcast.135) | data formatting | bytes 524288 | tf_op jit(solution)/shard_map/all_to_all | solution.py:95
  149.8 48.9 %while.19 = (s32[]{:T(128)}, bf16[256,2,8,32]{0,3,2,1:T(8,128)(2,1)S(1)}, f32[256,2,8,64]{0,3,2,1:T(8,128)}, bf16[256,2,8,64]{0,3,2,1:T(8,128)(2,1)}, pred[]{:T(...) while((s32[]{:T(128)}, ...), condition=%wide.region_1.2_spmd, body=%wide.region_0.1_spmd.sunk | while | flops 4456468 | bytes 4358505 | solution.py:119
  151.1 3.9 %collective-permute-done = bf16[256,2,8,32]{0,3,2,1:T(8,128)(2,1)S(1)} collective-permute-done((bf16[256,2,8,32]{0,3,2,1:T(8,128)(2,1)S(1)}, bf16[256,2,8,32]{0,3,2,1:T(8,128)(2,1)S(1)}, u32[]{:S(2)}, u32[]{:S(2)}) %collective-permute-start) | collective-permute-done | bytes 262176 | tf_op jit(solution)/shard_map/while/body/eval_jaxpr/ppermute | solution.py:31
  160.2 3.7 %collective-permute-start = (bf16[256,2,8,32]{0,3,2,1:T(8,128)(2,1)S(1)}, bf16[256,2,8,32]{0,3,2,1:T(8,128)(2,1)S(1)}, u32[]{:S(2)}, u32[]{:S(2)}) collective-permute-start(bf16[256,2,8,32]{0,3,2,1:T(8,128)(2,1)S(1)} %get-tuple-element.346), channel_id=1, source_target_pairs={{0,28},{4,0},{8,4},{12,8},{16,12},{20,16},{24,20},{28,24},{1,29},{... | collective-permute-start | bytes 786440 | tf_op jit(solution)/shard_map/while/body/eval_jaxpr/ppermute | solution.py:31
  163.9 3.9 %collective-permute-done = bf16[256,2,8,32]{0,3,2,1:T(8,128)(2,1)S(1)} collective-permute-done((bf16[256,2,8,32]{0,3,2,1:T(8,128)(2,1)S(1)}, bf16[256,2,8,32]{0,3,2,1:T(8,128)(2,1)S(1)}, u32[]{:S(2)}, u32[]{:S(2)}) %collective-permute-start) | collective-permute-done | bytes 262176 | tf_op jit(solution)/shard_map/while/body/eval_jaxpr/ppermute | solution.py:31
  173.0 3.7 %collective-permute-start = (bf16[256,2,8,32]{0,3,2,1:T(8,128)(2,1)S(1)}, bf16[256,2,8,32]{0,3,2,1:T(8,128)(2,1)S(1)}, u32[]{:S(2)}, u32[]{:S(2)}) collective-permute-start(bf16[256,2,8,32]{0,3,2,1:T(8,128)(2,1)S(1)} %get-tuple-element.346), channel_id=1, source_target_pairs={{0,28},{4,0},{8,4},{12,8},{16,12},{20,16},{24,20},{28,24},{1,29},{... | collective-permute-start | bytes 786440 | tf_op jit(solution)/shard_map/while/body/eval_jaxpr/ppermute | solution.py:31
  176.8 3.9 %collective-permute-done = bf16[256,2,8,32]{0,3,2,1:T(8,128)(2,1)S(1)} collective-permute-done((bf16[256,2,8,32]{0,3,2,1:T(8,128)(2,1)S(1)}, bf16[256,2,8,32]{0,3,2,1:T(8,128)(2,1)S(1)}, u32[]{:S(2)}, u32[]{:S(2)}) %collective-permute-start) | collective-permute-done | bytes 262176 | tf_op jit(solution)/shard_map/while/body/eval_jaxpr/ppermute | solution.py:31
  185.8 3.8 %collective-permute-start = (bf16[256,2,8,32]{0,3,2,1:T(8,128)(2,1)S(1)}, bf16[256,2,8,32]{0,3,2,1:T(8,128)(2,1)S(1)}, u32[]{:S(2)}, u32[]{:S(2)}) collective-permute-start(bf16[256,2,8,32]{0,3,2,1:T(8,128)(2,1)S(1)} %get-tuple-element.346), channel_id=1, source_target_pairs={{0,28},{4,0},{8,4},{12,8},{16,12},{20,16},{24,20},{28,24},{1,29},{... | collective-permute-start | bytes 786440 | tf_op jit(solution)/shard_map/while/body/eval_jaxpr/ppermute | solution.py:31
  189.6 3.9 %collective-permute-done = bf16[256,2,8,32]{0,3,2,1:T(8,128)(2,1)S(1)} collective-permute-done((bf16[256,2,8,32]{0,3,2,1:T(8,128)(2,1)S(1)}, bf16[256,2,8,32]{0,3,2,1:T(8,128)(2,1)S(1)}, u32[]{:S(2)}, u32[]{:S(2)}) %collective-permute-start) | collective-permute-done | bytes 262176 | tf_op jit(solution)/shard_map/while/body/eval_jaxpr/ppermute | solution.py:31
  200.0 4.6 %collective-permute-start.6 = (bf16[256,2,8,8]{0,3,2,1:T(8,128)(2,1)S(1)}, bf16[256,2,8,8]{0,3,2,1:T(8,128)(2,1)S(1)}, u32[]{:S(2)}, u32[]{:S(2)}) collective-permute-start(bf16[256,2,8,8]{0,3,2,1:T(8,128)(2,1)S(1)} %get-tuple-element.252), channel_id=1, source_target_pairs={{0,16},{4,20},{8,24},{12,28},{16,0},{20,4},{24,8},{28,12},{1,17},{... | collective-permute-start | bytes 196616 | tf_op jit(solution)/shard_map/ppermute | solution.py:127
  (104 shorter events, 47.4 us)
Async XLA Ops:
  0.0 99.4 %collective-permute-start.1 = (bf16[8,8,2,1024]{3,2,1,0:T(2,128)(2,1)}, bf16[8,8,2,1024]{3,2,1,0:T(2,128)(2,1)S(1)}, u32[]{:S(2)}, u32[]{:S(2)}) collective-permute-start(bf16[8,8,2,1024]{3,2,1,0:T(2,128)(2,1)} %param.4), channel_id=1, source_target_pairs={{0,1},{1,2},{2,3},{4,5},{5,6},{6,7},{8,9},{9,10},{10,11},{12,13},{... | collective-permute-start | bytes 786440 | tf_op jit(solution)/shard_map/ppermute | solution.py:25
  6.0 93.2 %collective-permute-start.2 = (bf16[8,7,2,1024]{3,2,1,0:T(2,128)(2,1)S(1)}, bf16[8,7,2,1024]{3,2,1,0:T(2,128)(2,1)S(1)}, u32[]{:S(2)}, u32[]{:S(2)}) collective-permute-start(bf16[8,7,2,1024]{3,2,1,0:T(2,128)(2,1)S(1)} %slice.151), channel_id=1, source_target_pairs={{0,2},{1,3},{4,6},{5,7},{8,10},{9,11},{12,14},{13,15},{16,18},{17,... | collective-permute-start | bytes 688136 | tf_op jit(solution)/shard_map/ppermute | solution.py:25
  85.0 14.2 %copy-start.3 = (f32[16,1024]{1,0:T(8,128)S(1)}, f32[16,1024]{1,0:T(8,128)}, u32[]{:S(2)}) copy-start(f32[16,1024]{1,0:T(8,128)} %param.5) | copy-start | bytes 196612
  85.0 14.9 %copy-start.2 = (bf16[8,8,2,1024]{3,2,1,0:T(2,128)(2,1)S(1)}, bf16[8,8,2,1024]{3,2,1,0:T(2,128)(2,1)}, u32[]{:S(2)}) copy-start(bf16[8,8,2,1024]{3,2,1,0:T(2,128)(2,1)} %param.4) | copy-start | bytes 786436
  123.4 8.8 %all-to-all-start = ((bf16[4,2,16384]{2,1,0:T(2,128)(2,1)}), bf16[4,2,16384]{2,1,0:T(2,128)(2,1)S(1)}, u32[]{:S(2)}, u32[]{:S(2)}) async-start(bf16[4,2,16384]{2,1,0:T(2,128)(2,1)} %reshape.208), calls=%async_computation | async-start | bytes 524288 | tf_op jit(solution)/shard_map/all_to_all | solution.py:95
  148.6 1.1 copy-start
  149.8 5.2 %collective-permute-start = (bf16[256,2,8,32]{0,3,2,1:T(8,128)(2,1)S(1)}, bf16[256,2,8,32]{0,3,2,1:T(8,128)(2,1)S(1)}, u32[]{:S(2)}, u32[]{:S(2)}) collective-permute-start(bf16[256,2,8,32]{0,3,2,1:T(8,128)(2,1)S(1)} %get-tuple-element.346), channel_id=1, source_target_pairs={{0,28},{4,0},{8,4},{12,8},{16,12},{20,16},{24,20},{28,24},{1,29},{... | collective-permute-start | bytes 786440 | tf_op jit(solution)/shard_map/while/body/eval_jaxpr/ppermute | solution.py:31
  160.2 7.6 %collective-permute-start = (bf16[256,2,8,32]{0,3,2,1:T(8,128)(2,1)S(1)}, bf16[256,2,8,32]{0,3,2,1:T(8,128)(2,1)S(1)}, u32[]{:S(2)}, u32[]{:S(2)}) collective-permute-start(bf16[256,2,8,32]{0,3,2,1:T(8,128)(2,1)S(1)} %get-tuple-element.346), channel_id=1, source_target_pairs={{0,28},{4,0},{8,4},{12,8},{16,12},{20,16},{24,20},{28,24},{1,29},{... | collective-permute-start | bytes 786440 | tf_op jit(solution)/shard_map/while/body/eval_jaxpr/ppermute | solution.py:31
  173.0 7.6 %collective-permute-start = (bf16[256,2,8,32]{0,3,2,1:T(8,128)(2,1)S(1)}, bf16[256,2,8,32]{0,3,2,1:T(8,128)(2,1)S(1)}, u32[]{:S(2)}, u32[]{:S(2)}) collective-permute-start(bf16[256,2,8,32]{0,3,2,1:T(8,128)(2,1)S(1)} %get-tuple-element.346), channel_id=1, source_target_pairs={{0,28},{4,0},{8,4},{12,8},{16,12},{20,16},{24,20},{28,24},{1,29},{... | collective-permute-start | bytes 786440 | tf_op jit(solution)/shard_map/while/body/eval_jaxpr/ppermute | solution.py:31
  185.8 7.6 %collective-permute-start = (bf16[256,2,8,32]{0,3,2,1:T(8,128)(2,1)S(1)}, bf16[256,2,8,32]{0,3,2,1:T(8,128)(2,1)S(1)}, u32[]{:S(2)}, u32[]{:S(2)}) collective-permute-start(bf16[256,2,8,32]{0,3,2,1:T(8,128)(2,1)S(1)} %get-tuple-element.346), channel_id=1, source_target_pairs={{0,28},{4,0},{8,4},{12,8},{16,12},{20,16},{24,20},{28,24},{1,29},{... | collective-permute-start | bytes 786440 | tf_op jit(solution)/shard_map/while/body/eval_jaxpr/ppermute | solution.py:31
  199.8 7.9 %collective-permute-start.3 = (bf16[256,2,8,8]{0,3,2,1:T(8,128)(2,1)S(1)}, bf16[256,2,8,8]{0,3,2,1:T(8,128)(2,1)S(1)}, u32[]{:S(2)}, u32[]{:S(2)}) collective-permute-start(bf16[256,2,8,8]{0,3,2,1:T(8,128)(2,1)S(1)} %get-tuple-element.255), channel_id=1, source_target_pairs={{0,4},{4,8},{8,12},{12,16},{16,20},{20,24},{24,28},{28,0},{1,5},{5... | collective-permute-start | bytes 196616 | tf_op jit(solution)/shard_map/ppermute | solution.py:127
  199.8 7.9 %collective-permute-start.4 = (bf16[256,2,8,8]{0,3,2,1:T(8,128)(2,1)S(1)}, bf16[256,2,8,8]{0,3,2,1:T(8,128)(2,1)S(1)}, u32[]{:S(2)}, u32[]{:S(2)}) collective-permute-start(bf16[256,2,8,8]{0,3,2,1:T(8,128)(2,1)S(1)} %get-tuple-element.254), channel_id=1, source_target_pairs={{0,8},{4,12},{8,16},{12,20},{16,24},{20,28},{24,0},{28,4},{1,9},{5... | collective-permute-start | bytes 196616 | tf_op jit(solution)/shard_map/ppermute | solution.py:127
  199.9 11.9 %collective-permute-start.5 = (bf16[256,2,8,8]{0,3,2,1:T(8,128)(2,1)S(1)}, bf16[256,2,8,8]{0,3,2,1:T(8,128)(2,1)S(1)}, u32[]{:S(2)}, u32[]{:S(2)}) collective-permute-start(bf16[256,2,8,8]{0,3,2,1:T(8,128)(2,1)S(1)} %get-tuple-element.253), channel_id=1, source_target_pairs={{0,12},{4,16},{8,20},{12,24},{16,28},{20,0},{24,4},{28,8},{1,13},{... | collective-permute-start | bytes 196616 | tf_op jit(solution)/shard_map/ppermute | solution.py:127
  200.0 12.0 %collective-permute-start.6 = (bf16[256,2,8,8]{0,3,2,1:T(8,128)(2,1)S(1)}, bf16[256,2,8,8]{0,3,2,1:T(8,128)(2,1)S(1)}, u32[]{:S(2)}, u32[]{:S(2)}) collective-permute-start(bf16[256,2,8,8]{0,3,2,1:T(8,128)(2,1)S(1)} %get-tuple-element.252), channel_id=1, source_target_pairs={{0,16},{4,20},{8,24},{12,28},{16,0},{20,4},{24,8},{28,12},{1,17},{... | collective-permute-start | bytes 196616 | tf_op jit(solution)/shard_map/ppermute | solution.py:127
  204.5 7.5 %collective-permute-start.7 = (bf16[256,2,8,8]{0,3,2,1:T(8,128)(2,1)S(1)}, bf16[256,2,8,8]{0,3,2,1:T(8,128)(2,1)S(1)}, u32[]{:S(2)}, u32[]{:S(2)}) collective-permute-start(bf16[256,2,8,8]{0,3,2,1:T(8,128)(2,1)S(1)} %get-tuple-element.251), channel_id=1, source_target_pairs={{0,20},{4,24},{8,28},{12,0},{16,4},{20,8},{24,12},{28,16},{1,21},{... | collective-permute-start | bytes 196616 | tf_op jit(solution)/shard_map/ppermute | solution.py:127
  207.7 6.5 %collective-permute-start.8 = (bf16[256,2,8,8]{0,3,2,1:T(8,128)(2,1)S(1)}, bf16[256,2,8,8]{0,3,2,1:T(8,128)(2,1)S(1)}, u32[]{:S(2)}, u32[]{:S(2)}) collective-permute-start(bf16[256,2,8,8]{0,3,2,1:T(8,128)(2,1)S(1)} %get-tuple-element.250), channel_id=1, source_target_pairs={{0,24},{4,28},{8,0},{12,4},{16,8},{20,12},{24,16},{28,20},{1,25},{... | collective-permute-start | bytes 196616 | tf_op jit(solution)/shard_map/ppermute | solution.py:127
  207.7 6.5 %collective-permute-start.9 = (bf16[256,2,8,8]{0,3,2,1:T(8,128)(2,1)S(1)}, bf16[256,2,8,8]{0,3,2,1:T(8,128)(2,1)S(1)}, u32[]{:S(2)}, u32[]{:S(2)}) collective-permute-start(bf16[256,2,8,8]{0,3,2,1:T(8,128)(2,1)S(1)} %get-tuple-element.249), channel_id=1, source_target_pairs={{0,28},{4,0},{8,4},{12,8},{16,12},{20,16},{24,20},{28,24},{1,29},{... | collective-permute-start | bytes 196616 | tf_op jit(solution)/shard_map/ppermute | solution.py:127
  214.2 1.2 copy-start.1
